TPU v7x, 128 devices: a whole 4x4x4 slice. The times are simulated.
128 devices in a mesh: sub: 16 (over y, z), grp: 8 (over x, core).
Axes of the slice: x: 4, y: 4, z: 4, core: 2. Of those that a mesh axis runs over, the one named last changes fastest.
Arguments:
- interior_res: bfloat16 [1024, 32, 256], P(('sub', 'grp')), may hold values from -6 to 6
- interface_res: bfloat16 [1024, 32, 512], P(('sub', 'grp')), may hold values from -6 to 6
- interior_inv: bfloat16 [1024, 256, 256], P(('sub', 'grp')), may hold values from -0.375 to 0.375
- coupling: bfloat16 [1024, 512, 256], P(('sub', 'grp')), may hold values from -0.375 to 0.375
- schur_inv: bfloat16 [1024, 512, 512], P(('sub', 'grp')), may hold values from -0.25 to 0.25
- coarse_inv: bfloat16 [512, 128, 128], P('grp'), may hold values from -0.5 to 0.5
- coarse_part: int32 [524288, 1], P(('sub', 'grp')), may hold values from 0 to 127; in each aligned block of 4096 rows (0 to 4095, 4096 to 8191, ...) at most 64 rows name the same one
- coarse_slot: int32 [524288], P(('sub', 'grp')), may hold values from 0 to 511
- live_count: int32 [1024], P(('sub', 'grp')), may hold values from 128 to 512
Outputs:
- interior_update: bfloat16 [1024, 32, 256], P(('sub', 'grp'))
- interface_update: bfloat16 [1024, 32, 512], P(('sub', 'grp'))
Inputs may be any that keep to these rules, and one draw needn't show every extreme that they name: `coarse_part`: in each device's aligned block of 4096 rows no section is named by more than 64 rows, a bound that some block reaches.
All inputs are finite; a program needn't handle non-finite values.
Results may differ from a plain program's by a relative error of at most 0.0076.
Values may be sent and summed in bfloat16 or wider, within the bound.
No kernel may reach another device: no remote copies, remote signals or barrier semaphores. Data moves between devices by JAX's collectives and lax.ppermute only.
A program may use at most 64 MiB of HBM per device.

v0:
```python
import math
import jax
import jax.numpy as jnp
from jax import lax
from jax.sharding import PartitionSpec as P


def coarse_apply(right_side, inverse_blocks):
    vec_count = right_side.shape[0]
    block_size = inverse_blocks.shape[1]
    reshaped = right_side.reshape(vec_count, -1, block_size)
    solved = jnp.einsum(
        "kbj,bij->kbi", reshaped, inverse_blocks, preferred_element_type=jnp.float32
    )
    return solved.reshape(vec_count, -1).astype(jnp.bfloat16)


def spread_cols(values, target, total):
    width = math.gcd(total, 512)

    def spread_one_block(number):
        columns = number * width + lax.iota(jnp.int32, width)
        table = (target[:, None] == columns[None, :]).astype(jnp.bfloat16)
        return jnp.dot(values, table, preferred_element_type=jnp.float32)

    blocks = lax.map(spread_one_block, jnp.arange(total // width, dtype=jnp.int32))
    return jnp.transpose(blocks, (1, 0, 2)).reshape(values.shape[0], total)


def pick_cols(values, wanted):
    count = wanted.shape[0]
    width = math.gcd(count, 512)
    source = lax.iota(jnp.int32, values.shape[1])

    def pick_one_block(number):
        chosen = lax.dynamic_slice_in_dim(wanted, number * width, width, 0)
        table = (source[:, None] == chosen[None, :]).astype(jnp.bfloat16)
        return jnp.dot(values, table, preferred_element_type=jnp.float32)

    blocks = lax.map(pick_one_block, jnp.arange(count // width, dtype=jnp.int32))
    return jnp.transpose(blocks, (1, 0, 2)).reshape(values.shape[0], count).astype(jnp.bfloat16)


def place_in_section(section_list, sections):
    rows_dev = section_list.shape[0]
    width = math.gcd(rows_dev, 128)
    section_hot = (section_list[:, None] == jnp.arange(sections, dtype=jnp.int32)[None, :]).astype(
        jnp.float32
    )
    hot_blocks = section_hot.reshape(rows_dev // width, width, sections)
    lower = (
        lax.broadcasted_iota(jnp.int32, (width, width), 0)
        >= lax.broadcasted_iota(jnp.int32, (width, width), 1)
    ).astype(jnp.float32)
    within = jnp.einsum("ij,bjs->bis", lower, hot_blocks, precision=lax.Precision.HIGHEST)
    totals = within[:, -1, :]
    before = jnp.cumsum(totals, axis=0) - totals
    counted = (within + before[:, None, :]).reshape(rows_dev, sections)
    return jnp.sum((counted - 1.0) * section_hot, axis=1).astype(jnp.int32)


def with_slots(flattened, slot_values):
    upper = (slot_values // 256).astype(jnp.bfloat16)[None, :]
    lower = (slot_values % 256).astype(jnp.bfloat16)[None, :]
    return jnp.concatenate([flattened, upper, lower], axis=0)


def read_slots(received, vec_count):
    upper = received[vec_count].astype(jnp.int32)
    lower = received[vec_count + 1].astype(jnp.int32)
    return (received[:vec_count], upper * 256 + lower)


def on_device(
    interior_res,
    interface_res,
    interior_inv,
    coupling,
    schur_inv,
    coarse_inv,
    coarse_part,
    coarse_slot,
    live_count,
):
    sub_count, vec_count, interior = interior_res.shape
    boundary = interface_res.shape[2]
    owners = lax.axis_size("grp")
    subgroups = lax.axis_size("sub")
    sections = owners * subgroups
    rows_dev = sub_count * boundary
    capacity = 2 * rows_dev // sections
    piece_size = rows_dev // 8
    per_owner = coarse_inv.shape[0] * coarse_inv.shape[1]
    interior_pre = jnp.einsum(
        "sij,skj->ski", interior_inv, interior_res, preferred_element_type=jnp.float32
    ).astype(jnp.bfloat16)
    condensed = interface_res.astype(jnp.float32) - jnp.einsum(
        "sbi,ski->skb", coupling, interior_pre, preferred_element_type=jnp.float32
    )
    alive_mask = (
        lax.broadcasted_iota(jnp.int32, (sub_count, 1, boundary), 2) < live_count[:, None, None]
    )
    condensed = jnp.where(alive_mask, condensed, 0.0).astype(jnp.bfloat16)
    section_list = coarse_part[:, 0]
    owner_list = section_list % owners
    piece_list = section_list // owners
    position = place_in_section(section_list, sections)
    flattened = jnp.transpose(condensed, (1, 0, 2)).reshape(vec_count, rows_dev)
    destination = owner_list * (subgroups * capacity) + piece_list * capacity + position
    owner_slot = piece_list * piece_size + coarse_slot
    outgoing = spread_cols(
        with_slots(flattened, owner_slot), destination, sections * capacity
    ).astype(jnp.bfloat16)
    received = lax.all_to_all(outgoing, "grp", split_axis=1, concat_axis=1, tiled=True)
    recv_rows, recv_slots = read_slots(received, vec_count)
    partial_sum = spread_cols(recv_rows, recv_slots, per_owner)
    summed = lax.psum(partial_sum, "sub")
    coarse_sol = coarse_apply(summed.astype(jnp.bfloat16), coarse_inv)
    replies = pick_cols(coarse_sol, recv_slots)
    returned = lax.all_to_all(replies, "grp", split_axis=1, concat_axis=1, tiled=True)
    correction = pick_cols(returned, destination)
    correction = jnp.transpose(correction.reshape(vec_count, sub_count, boundary), (1, 0, 2))
    local_term = jnp.einsum(
        "sbc,skc->skb", schur_inv, condensed, preferred_element_type=jnp.float32
    )
    interface_update = jnp.where(
        alive_mask, local_term + correction.astype(jnp.float32), 0.0
    ).astype(jnp.bfloat16)
    extended = interior_res.astype(jnp.float32) - jnp.einsum(
        "sbi,skb->ski", coupling, interface_update, preferred_element_type=jnp.float32
    )
    interior_update = jnp.einsum(
        "sij,skj->ski",
        interior_inv,
        extended.astype(jnp.bfloat16),
        preferred_element_type=jnp.float32,
    ).astype(jnp.bfloat16)
    return (interior_update, interface_update)


def solution(mesh):
    in_specs = (
        P(("sub", "grp"), None, None),
        P(("sub", "grp"), None, None),
        P(("sub", "grp"), None, None),
        P(("sub", "grp"), None, None),
        P(("sub", "grp"), None, None),
        P("grp", None, None),
        P(("sub", "grp"), None),
        P(("sub", "grp")),
        P(("sub", "grp")),
    )
    out_specs = (P(("sub", "grp"), None, None), P(("sub", "grp"), None, None))
    return jax.shard_map(
        on_device, mesh=mesh, in_specs=in_specs, out_specs=out_specs, check_vma=False
    )
```

profile of v0, /device:TPU:1, one launch (start us, length us, event | category | flops | bytes accessed | tf_op | source)
XLA Modules:
  0.0 473.6 jit_solution(12313746118868401771)
XLA Ops:
  10.9 69.0 %while.46 = (s32[]{:T(128)}, bf16[16,34,512]{2,1,0:T(8,128)(2,1)}, s32[4096]{0:T(1024)}, s32[16]{0:T(128)S(1)}, bf16[34,4096]{1,0:T(8,128)(2,1)}, /*index=5*/s32[1]{0:T(128)}) while((s32[]{:T(128)}, bf16[16,34,512]{2,1,0:T(8,128)(2,1)}, s32[4096]{0:T(1024)}, s32[16]{0:T(128)S(1)}, bf16[34,4096]{1,0:T(8,128)(2,1)}, ...), condition=%wide.region_3.4_spmd.clone, body=%wide.region_2.3_spmd.sunk.clone | while | flops 144704000 | bytes 430689 | solution.py:26
  12.2 3.1 fusion.94
  16.5 3.1 fusion.94
  20.8 3.1 fusion.94
  25.1 3.1 fusion.94
  29.4 3.1 fusion.94
  33.7 3.1 fusion.94
  38.0 3.1 fusion.94
  42.3 3.1 fusion.94
  51.0 3.1 fusion.94
  55.3 3.1 fusion.94
  59.6 3.1 fusion.94
  68.2 3.1 fusion.94
  72.5 3.1 fusion.94
  86.2 5.8 %all-to-all-start = ((bf16[34,8,1024]{2,0,1:T(8,128)(2,1)}), bf16[34,8,1024]{2,0,1:T(8,128)(2,1)}, u32[]{:S(2)}, u32[]{:S(2)}) async-start(bf16[34,8,1024]{2,0,1:T(8,128)(2,1)} %copy.27), calls=%async_computation | async-start | bytes 1310720 | tf_op jit(solution)/shard_map/all_to_all | solution.py:114
  92.8 10.0 %all-to-all-done = bf16[34,8,1024]{2,0,1:T(8,128)(2,1)} async-done(((bf16[34,8,1024]{2,0,1:T(8,128)(2,1)}), bf16[34,8,1024]{2,0,1:T(8,128)(2,1)}, u32[]{:S(2)}, u32[]{:S(2)}) %all-to-all-start) | async-done | bytes 557088 | tf_op jit(solution)/shard_map/all_to_all | solution.py:114
  106.5 88.7 %while.47 = (s32[]{:T(128)}, f32[16,32,512]{2,1,0:T(8,128)}, s32[8192]{0:T(1024)}, s32[16]{0:T(128)S(1)}, bf16[32,8192]{1,0:T(8,128)(2,1)}, /*index=5*/s32[1]{0:T(128)}) while((s32[]{:T(128)}, f32[16,32,512]{2,1,0:T(8,128)}, s32[8192]{0:T(1024)}, s32[16]{0:T(128)S(1)}, bf16[32,8192]{1,0:T(8,128)(2,1)}, /*index=5*/s32[1]{0:T(128)}) %tuple.96), condition=%wide.region_5.6_spmd.clone, body=%wide.region_4.5_spmd.sunk.clone | while | flops 272630272 | bytes 627297 | solution.py:26
  107.7 4.4 fusion.97
  113.2 4.4 fusion.97
  118.8 4.4 fusion.97
  124.3 4.4 fusion.97
  129.9 4.4 fusion.97
  135.4 4.4 fusion.97
  140.9 4.4 fusion.97
  146.5 4.4 fusion.97
  152.0 4.4 fusion.97
  157.6 4.4 fusion.97
  163.1 4.4 fusion.97
  168.7 4.4 fusion.97
  174.2 4.4 fusion.97
  179.8 4.4 fusion.97
  185.3 4.4 fusion.97
  190.9 4.4 fusion.97
  197.6 76.3 %all-reduce.1 = bf16[32,8192]{1,0:T(8,128)(2,1)} all-reduce(f32[32,8192]{1,0:T(8,128)} %bitcast.120), channel_id=1, replica_groups=mesh['sub'=16,'grp'=8] {'sub'}, use_global_device_ids=true, to_apply=%region_6.7 | all-reduce | flops 262144 | bytes 1572864 | tf_op jit(solution)/shard_map/psum | solution.py:117
  277.0 101.6 %while.48 = (s32[]{:T(128)}, bf16[16,32,512]{2,1,0:T(8,128)(2,1)}, s32[16]{0:T(128)S(1)}, s32[8192]{0:T(1024)}, bf16[32,8192]{1,0:T(8,128)(2,1)}, /*index=5*/s32[1]{0:T(128)}) while((s32[]{:T(128)}, bf16[16,32,512]{2,1,0:T(8,128)(2,1)}, s32[16]{0:T(128)S(1)}, s32[8192]{0:T(1024)}, bf16[32,8192]{1,0:T(8,128)(2,1)}, ...), condition=%wide.region_8.9_spmd.clone.clone, body=%wide.region_7.8_spmd.clone.sunk.clone | while | flops 272629760 | bytes 596611 | solution.py:40
  279.0 4.4 fusion.99
  285.4 4.4 fusion.99
  291.7 4.4 fusion.99
  298.1 4.4 fusion.99
  304.4 4.4 fusion.99
  310.8 4.4 fusion.99
  317.1 4.4 fusion.99
  323.5 4.4 fusion.99
  329.8 4.4 fusion.99
  336.2 4.4 fusion.99
  342.5 4.4 fusion.99
  348.9 4.4 fusion.99
  355.2 4.4 fusion.99
  361.6 4.4 fusion.99
  367.9 4.4 fusion.99
  374.3 4.4 fusion.99
  384.9 19.1 %all-to-all-start.1 = ((bf16[32,8,1024]{2,0,1:T(8,128)(2,1)}), bf16[32,8,1024]{2,0,1:T(8,128)(2,1)}, u32[]{:S(2)}, u32[]{:S(2)}) async-start(bf16[32,8,1024]{2,0,1:T(8,128)(2,1)} %copy.33), calls=%async_computation.1 | async-start | bytes 1048576 | tf_op jit(solution)/shard_map/all_to_all | solution.py:120
  404.0 9.5 %all-to-all-done.1 = bf16[32,8,1024]{2,0,1:T(8,128)(2,1)} async-done(((bf16[32,8,1024]{2,0,1:T(8,128)(2,1)}), bf16[32,8,1024]{2,0,1:T(8,128)(2,1)}, u32[]{:S(2)}, u32[]{:S(2)}) %all-to-all-start.1) | async-done | bytes 524320 | tf_op jit(solution)/shard_map/all_to_all | solution.py:120
  415.3 50.9 %while.49 = (s32[]{:T(128)}, bf16[8,32,512]{2,1,0:T(8,128)(2,1)}, s32[8]{0:T(128)S(1)}, s32[4096]{0:T(1024)}, bf16[32,8192]{1,0:T(8,128)(2,1)}, /*index=5*/s32[1]{0:T(128)}) while((s32[]{:T(128)}, bf16[8,32,512]{2,1,0:T(8,128)(2,1)}, s32[8]{0:T(128)S(1)}, s32[4096]{0:T(1024)}, bf16[32,8192]{1,0:T(8,128)(2,1)}, ...), condition=%wide.region_10.11_spmd.clone.clone, body=%wide.region_9.10_spmd.clone.sunk.clone | while | flops 272629760 | bytes 596611 | solution.py:40
  417.3 4.4 fusion.101
  423.7 4.4 fusion.101
  430.0 4.4 fusion.101
  436.4 4.4 fusion.101
  442.8 4.4 fusion.101
  449.1 4.4 fusion.101
  455.5 4.4 fusion.101
  461.9 4.4 fusion.101
  466.2 4.2 fusion.37
  470.5 3.1 convolution_convert_fusion.1
  (161 shorter events, 94.8 us)
Async XLA Ops:
  0.6 273.3 %copy-start = (bf16[64,128,128]{2,1,0:T(8,128)(2,1)S(1)}, bf16[64,128,128]{2,1,0:T(8,128)(2,1)}, u32[]{:S(2)}) copy-start(bf16[64,128,128]{2,1,0:T(8,128)(2,1)} %param.22) | copy-start | bytes 6291460
  0.6 1.8 copy-start.3
  0.7 3.1 copy-start.5
  0.7 4.4 copy-start.6
  0.7 5.0 %copy-start.1 = (bf16[8,256,256]{2,1,0:T(8,128)(2,1)S(1)}, bf16[8,256,256]{2,1,0:T(8,128)(2,1)}, u32[]{:S(2)}) copy-start(bf16[8,256,256]{2,1,0:T(8,128)(2,1)} %param.19) | copy-start | bytes 3145732
  0.7 5.0 %copy-start.2 = (bf16[8,32,256]{2,1,0:T(8,128)(2,1)S(1)}, bf16[8,32,256]{2,1,0:T(8,128)(2,1)}, u32[]{:S(2)}) copy-start(bf16[8,32,256]{2,1,0:T(8,128)(2,1)} %param.17) | copy-start | bytes 393220
  86.2 16.6 %all-to-all-start = ((bf16[34,8,1024]{2,0,1:T(8,128)(2,1)}), bf16[34,8,1024]{2,0,1:T(8,128)(2,1)}, u32[]{:S(2)}, u32[]{:S(2)}) async-start(bf16[34,8,1024]{2,0,1:T(8,128)(2,1)} %copy.27), calls=%async_computation | async-start | bytes 1310720 | tf_op jit(solution)/shard_map/all_to_all | solution.py:114
  384.9 28.5 %all-to-all-start.1 = ((bf16[32,8,1024]{2,0,1:T(8,128)(2,1)}), bf16[32,8,1024]{2,0,1:T(8,128)(2,1)}, u32[]{:S(2)}, u32[]{:S(2)}) async-start(bf16[32,8,1024]{2,0,1:T(8,128)(2,1)} %copy.33), calls=%async_computation.1 | async-start | bytes 1048576 | tf_op jit(solution)/shard_map/all_to_all | solution.py:120
  415.3 50.9 %copy-start.4 = (pred[8,512]{1,0:T(8,128)(4,1)S(1)}, pred[8,512]{1,0:T(8,128)(4,1)}, u32[]{:S(2)}) copy-start(pred[8,512]{1,0:T(8,128)(4,1)} %iota_compare_fusion.17) | copy-start | bytes 12292
where the time goes:
time: 477 us; the launch traced here: 474 us
  matrix products  238 us (50%)
  blocking collectives  76.3 us (16%)
  local copies, waits for them, and re-layouts  71.9 us (15%)
  loops' own time  35.1 us (7%)
  starting transfers between devices  24.8 us (5%)
  waiting for transfers between devices  19.5 us (4%)
  other arithmetic  7.01 us (1%)
    dot_general x32, matrix products, spread_one_block(): return jnp.dot(values, table, preferred_element_type=jnp.float32)  119 us
    dot_general x24, matrix products, pick_one_block(): return jnp.dot(values, table, preferred_element_type=jnp.float32)  105 us
    psum x1, blocking collectives, on_device(): summed = lax.psum(partial_sum, 'sub')  76.3 us
    dynamic_slice x48, local copies, waits for them, and re-layouts, spread_cols(): lax.map(spread_one_block, jnp.arange(total // width, dtype=jnp.int32))  28 us
    another operation x2, loops' own time, spread_cols(): lax.map(spread_one_block, jnp.arange(total // width, dtype=jnp.int32))  19.7 us
    all_to_all x1, starting transfers between devices, on_device(): lax.all_to_all(replies, 'grp', split_axis=1, concat_axis=1, tiled=True)  19.1 us
    dynamic_slice x24, local copies, waits for them, and re-layouts, pick_one_block(): chosen = lax.dynamic_slice_in_dim(wanted, number * width, width, 0)  18.2 us
    another operation x2, loops' own time, pick_cols(): lax.map(pick_one_block, jnp.arange(count // width, dtype=jnp.int32))  15.4 us
  transfers between devices with their start and end apart: 2, of which 2 were waited for; matrix products, arithmetic and copies ran while one was open for 0% of the time, Pallas kernels for 0%

commit v1 on v0

--- a/solution.py
+++ b/solution.py
@@ -114,7 +114,7 @@
     received = lax.all_to_all(outgoing, "grp", split_axis=1, concat_axis=1, tiled=True)
     recv_rows, recv_slots = read_slots(received, vec_count)
     partial_sum = spread_cols(recv_rows, recv_slots, per_owner)
-    summed = lax.psum(partial_sum, "sub")
+    summed = jnp.sum(jax.lax.all_gather(partial_sum, "sub"), 0)
     coarse_sol = coarse_apply(summed.astype(jnp.bfloat16), coarse_inv)
     replies = pick_cols(coarse_sol, recv_slots)
     returned = lax.all_to_all(replies, "grp", split_axis=1, concat_axis=1, tiled=True)

time: 477 us -> 524 us (1.099)
  waiting for transfers between devices: 19.5 us -> 132 us
  blocking collectives: 76.3 us -> 0 us
  starting transfers between devices: 24.8 us -> 10.9 us
  between operations: 0.76 us -> 14.1 us
  other arithmetic: 7.01 us -> 14.6 us
    all_gather x0 -> x1, waiting for transfers between devices: none -> 111 us  [on_device(): summed = jnp.sum(jax.lax.all_gather(partial_sum, 'sub'), 0)]
    psum x1 -> x0, blocking collectives: 76.3 us -> none  [on_device(): summed = lax.psum(partial_sum, 'sub')]
    all_to_all x1, starting transfers between devices: 19.1 us -> 5.09 us  [on_device(): lax.all_to_all(replies, 'grp', split_axis=1, concat_axis=1, tiled=True)]
    reduce_sum x0 -> x1, other arithmetic: none -> 7.51 us  [on_device(): summed = jnp.sum(jax.lax.all_gather(partial_sum, 'sub'), 0)]
  transfers between devices with their start and end apart: 2 -> 3, of which waited for: 2 -> 3; matrix products, arithmetic and copies ran while one was open for 0% -> 0% of each run, Pallas kernels for 0% -> 0%
where the time goes in v1:
time: 524 us; the launch traced here: 520 us
  matrix products  238 us (45%)
  waiting for transfers between devices  132 us (25%)
  local copies, waits for them, and re-layouts  75.3 us (14%)
  loops' own time  35.6 us (7%)
  other arithmetic  14.6 us (3%)
  between operations  14.1 us (3%)
  starting transfers between devices  10.9 us (2%)
    dot_general x32, matrix products, spread_one_block(): return jnp.dot(values, table, preferred_element_type=jnp.float32)  119 us
    all_gather x1, waiting for transfers between devices, on_device(): summed = jnp.sum(jax.lax.all_gather(partial_sum, 'sub'), 0)  111 us
    dot_general x24, matrix products, pick_one_block(): return jnp.dot(values, table, preferred_element_type=jnp.float32)  105 us
    dynamic_slice x48, local copies, waits for them, and re-layouts, spread_cols(): lax.map(spread_one_block, jnp.arange(total // width, dtype=jnp.int32))  28.5 us
    another operation x2, loops' own time, spread_cols(): lax.map(spread_one_block, jnp.arange(total // width, dtype=jnp.int32))  20.9 us
    dynamic_slice x24, local copies, waits for them, and re-layouts, pick_one_block(): chosen = lax.dynamic_slice_in_dim(wanted, number * width, width, 0)  18.3 us
    another operation x2, loops' own time, pick_cols(): lax.map(pick_one_block, jnp.arange(count // width, dtype=jnp.int32))  14.7 us
    all_to_all x1, waiting for transfers between devices, on_device(): lax.all_to_all(outgoing, 'grp', split_axis=1, concat_axis=1, tiled=True)  10.9 us
  transfers between devices with their start and end apart: 3, of which 3 were waited for; matrix products, arithmetic and copies ran while one was open for 0% of the time, Pallas kernels for 0%

profile of v1, /device:TPU:1, one launch (start us, length us, event | category | flops | bytes accessed | tf_op | source)
XLA Modules:
  0.0 520.5 jit_solution(7571896004683294192)
XLA Ops:
  17.4 69.0 %while.46 = (s32[]{:T(128)}, bf16[16,34,512]{2,1,0:T(8,128)(2,1)}, s32[4096]{0:T(1024)}, s32[16]{0:T(128)S(1)}, bf16[34,4096]{1,0:T(8,128)(2,1)}, /*index=5*/s32[1]{0:T(128)}) while((s32[]{:T(128)}, bf16[16,34,512]{2,1,0:T(8,128)(2,1)}, s32[4096]{0:T(1024)}, s32[16]{0:T(128)S(1)}, bf16[34,4096]{1,0:T(8,128)(2,1)}, ...), condition=%wide.region_3.4_spmd.clone, body=%wide.region_2.3_spmd.sunk.clone | while | flops 144704000 | bytes 430689 | solution.py:26
  18.7 3.1 fusion.94
  23.0 3.1 fusion.94
  27.3 3.1 fusion.94
  31.6 3.1 fusion.94
  44.6 3.1 fusion.94
  53.2 3.1 fusion.94
  57.5 3.1 fusion.94
  66.1 3.1 fusion.94
  70.4 3.1 fusion.94
  74.8 3.1 fusion.94
  79.1 3.1 fusion.94
  83.4 3.1 fusion.94
  92.7 5.8 %all-to-all-start = ((bf16[34,8,1024]{2,0,1:T(8,128)(2,1)}), bf16[34,8,1024]{2,0,1:T(8,128)(2,1)}, u32[]{:S(2)}, u32[]{:S(2)}) async-start(bf16[34,8,1024]{2,0,1:T(8,128)(2,1)} %copy.27), calls=%async_computation | async-start | bytes 1310720 | tf_op jit(solution)/shard_map/all_to_all | solution.py:114
  98.5 10.9 %all-to-all-done = bf16[34,8,1024]{2,0,1:T(8,128)(2,1)} async-done(((bf16[34,8,1024]{2,0,1:T(8,128)(2,1)}), bf16[34,8,1024]{2,0,1:T(8,128)(2,1)}, u32[]{:S(2)}, u32[]{:S(2)}) %all-to-all-start) | async-done | bytes 557088 | tf_op jit(solution)/shard_map/all_to_all | solution.py:114
  113.0 90.5 %while.47 = (s32[]{:T(128)}, f32[16,32,512]{2,1,0:T(8,128)}, s32[8192]{0:T(1024)}, s32[16]{0:T(128)S(1)}, bf16[32,8192]{1,0:T(8,128)(2,1)}, /*index=5*/s32[1]{0:T(128)}) while((s32[]{:T(128)}, f32[16,32,512]{2,1,0:T(8,128)}, s32[8192]{0:T(1024)}, s32[16]{0:T(128)S(1)}, bf16[32,8192]{1,0:T(8,128)(2,1)}, /*index=5*/s32[1]{0:T(128)}) %tuple.98), condition=%wide.region_5.6_spmd.clone, body=%wide.region_4.5_spmd.sunk.clone | while | flops 272630272 | bytes 627297 | solution.py:26
  114.3 4.4 fusion.97
  120.0 4.4 fusion.97
  125.6 4.4 fusion.97
  131.3 4.4 fusion.97
  136.9 4.4 fusion.97
  142.6 4.4 fusion.97
  148.3 4.4 fusion.97
  153.9 4.4 fusion.97
  159.6 4.4 fusion.97
  165.2 4.4 fusion.97
  170.9 4.4 fusion.97
  176.6 4.4 fusion.97
  182.2 4.4 fusion.97
  187.9 4.4 fusion.97
  193.5 4.4 fusion.97
  199.2 4.4 fusion.97
  209.8 111.3 %all-gather.2.cloned.1.call-done = f32[16,32,8192]{2,1,0:T(8,128)} async-done(((f32[1,32,8192]{2,1,0:T(8,128)}), f32[16,32,8192]{2,1,0:T(8,128)}) %all-gather.2.cloned.1.call-update) | async-done | bytes 16777232 | tf_op jit(solution)/shard_map/all_gather | solution.py:117
  321.0 7.5 %reduce_sum.19 = bf16[32,8192]{1,0:T(8,128)(2,1)} reduce(f32[16,32,8192]{2,1,0:T(8,128)} %all-gather.2.cloned.1.call-done, f32[]{:T(128)} %constant.99.clone.1), dimensions={0}, to_apply=%region_6.7 | reduce | flops 3932160 | bytes 17301508 | tf_op jit(solution)/shard_map/reduce_sum | solution.py:117
  331.7 101.0 %while.48 = (s32[]{:T(128)}, bf16[16,32,512]{2,1,0:T(8,128)(2,1)}, s32[16]{0:T(128)S(1)}, s32[8192]{0:T(1024)}, bf16[32,8192]{1,0:T(8,128)(2,1)}, /*index=5*/s32[1]{0:T(128)}) while((s32[]{:T(128)}, bf16[16,32,512]{2,1,0:T(8,128)(2,1)}, s32[16]{0:T(128)S(1)}, s32[8192]{0:T(1024)}, bf16[32,8192]{1,0:T(8,128)(2,1)}, ...), condition=%wide.region_8.9_spmd.clone.clone, body=%wide.region_7.8_spmd.clone.sunk.clone | while | flops 272629760 | bytes 596611 | solution.py:40
  333.6 4.4 fusion.99
  339.9 4.4 fusion.99
  346.2 4.4 fusion.99
  352.5 4.4 fusion.99
  358.8 4.4 fusion.99
  365.2 4.4 fusion.99
  371.5 4.4 fusion.99
  377.8 4.4 fusion.99
  384.1 4.4 fusion.99
  390.4 4.4 fusion.99
  396.7 4.4 fusion.99
  403.0 4.4 fusion.99
  409.3 4.4 fusion.99
  415.7 4.4 fusion.99
  422.0 4.4 fusion.99
  428.3 4.4 fusion.99
  438.9 5.1 all-to-all-start.1
  444.0 9.5 %all-to-all-done.1 = bf16[32,8,1024]{2,0,1:T(8,128)(2,1)} async-done(((bf16[32,8,1024]{2,0,1:T(8,128)(2,1)}), bf16[32,8,1024]{2,0,1:T(8,128)(2,1)}, u32[]{:S(2)}, u32[]{:S(2)}) %all-to-all-start.1) | async-done | bytes 524320 | tf_op jit(solution)/shard_map/all_to_all | solution.py:120
  455.3 50.9 %while.49 = (s32[]{:T(128)}, bf16[8,32,512]{2,1,0:T(8,128)(2,1)}, s32[8]{0:T(128)S(1)}, s32[4096]{0:T(1024)}, bf16[32,8192]{1,0:T(8,128)(2,1)}, /*index=5*/s32[1]{0:T(128)}) while((s32[]{:T(128)}, bf16[8,32,512]{2,1,0:T(8,128)(2,1)}, s32[8]{0:T(128)S(1)}, s32[4096]{0:T(1024)}, bf16[32,8192]{1,0:T(8,128)(2,1)}, ...), condition=%wide.region_10.11_spmd.clone.clone, body=%wide.region_9.10_spmd.clone.sunk.clone | while | flops 272629760 | bytes 596611 | solution.py:40
  457.3 4.4 fusion.101
  463.7 4.4 fusion.101
  470.1 4.4 fusion.101
  476.4 4.4 fusion.101
  482.8 4.4 fusion.101
  489.2 4.4 fusion.101
  495.5 4.4 fusion.101
  501.9 4.4 fusion.101
  506.3 4.2 fusion.37
  510.5 3.1 convolution_convert_fusion.1
  (165 shorter events, 101.3 us)
Async XLA Ops:
  7.2 321.4 %copy-start = (bf16[64,128,128]{2,1,0:T(8,128)(2,1)S(1)}, bf16[64,128,128]{2,1,0:T(8,128)(2,1)}, u32[]{:S(2)}) copy-start(bf16[64,128,128]{2,1,0:T(8,128)(2,1)} %param.22) | copy-start | bytes 6291460
  7.2 1.8 copy-start.3
  7.2 3.1 copy-start.5
  7.2 4.4 copy-start.6
  7.2 5.0 copy-start.1
  7.2 5.0 copy-start.2
  92.7 16.6 %all-to-all-start = ((bf16[34,8,1024]{2,0,1:T(8,128)(2,1)}), bf16[34,8,1024]{2,0,1:T(8,128)(2,1)}, u32[]{:S(2)}, u32[]{:S(2)}) async-start(bf16[34,8,1024]{2,0,1:T(8,128)(2,1)} %copy.27), calls=%async_computation | async-start | bytes 1310720 | tf_op jit(solution)/shard_map/all_to_all | solution.py:114
  98.5 222.5 %all-gather.2.cloned.1.call-start = ((), (), s32[]{:S(2)}) async-start(), calls=%async_computation.2 | async-start | bytes 17825792 | tf_op jit(solution)/shard_map/all_gather | solution.py:117
  438.9 14.5 %all-to-all-start.1 = ((bf16[32,8,1024]{2,0,1:T(8,128)(2,1)}), bf16[32,8,1024]{2,0,1:T(8,128)(2,1)}, u32[]{:S(2)}, u32[]{:S(2)}) async-start(bf16[32,8,1024]{2,0,1:T(8,128)(2,1)} %copy.33), calls=%async_computation.1 | async-start | bytes 1048576 | tf_op jit(solution)/shard_map/all_to_all | solution.py:120
  455.3 51.0 %copy-start.4 = (pred[8,512]{1,0:T(8,128)(4,1)S(1)}, pred[8,512]{1,0:T(8,128)(4,1)}, u32[]{:S(2)}) copy-start(pred[8,512]{1,0:T(8,128)(4,1)} %iota_compare_fusion.17) | copy-start | bytes 12292
Sparse Core Ops, SparseCore 0:
  209.0 111.9 all-gather.1
